TPU v7x, 32 devices: a whole 2x2x4 slice. The times are simulated.
32 devices in a mesh: site: 8 (over y, x, core), scen: 4 (over z).
Axes of the slice: x: 2, y: 2, z: 4, core: 2. Of those that a mesh axis runs over, the one named last changes fastest.
Arguments:
- normals: bfloat16 [20480, 1344], P('site', 'scen'), may hold values from -6 to 6
- pattern: int32 [32, 40], replicated, may hold values from 0 to 79, as said below
- factor: bfloat16 [32, 40, 256, 256], P('site', None, 'scen'), may hold values from -0.0625 to 0.0625
- temporal: bfloat16 [168, 168], replicated, may hold values from -0.5 to 0.5
- capacity: float32 [8192], P('site'), may hold values from 0.05 to 0.4
- spread: float32 [8192], P('site'), may hold values from 0.2 to 0.8
- bus_map: int32 [8192], replicated, may hold values from 0 to 511
Outputs:
- bus_power: float32 [512, 1344], P('site', 'scen')
Inputs may be any that keep to these rules, and one draw needn't show every extreme that they name: `pattern`: each block row names 40 different column blocks. The 4 block rows of one index of site (rows k * 4 to (k + 1) * 4 - 1) name at most 5 different column blocks among those held by any one index of site (blocks j * 10 to (j + 1) * 10 - 1), and exactly 5 among those held by index k itself.
All inputs are finite; a program needn't handle non-finite values.
Results may differ from a plain program's by a relative error of at most 0.0013.
Values may be sent and summed in bfloat16 or wider, within the bound.
A program may use at most 192 MiB of HBM per device.

v0:
```python
import jax
import jax.numpy as jnp
from jax import lax
from jax.sharding import PartitionSpec as P

BLK = 256
HOURS = 168
NZ = 40
MAX_COLUMN_BLOCKS = 5
RB_DEV = 4
BUS_DEV = 64


def shards(normals, pattern, factor, temporal, capacity, spread, bus_map):
    own_index = lax.axis_index("site")
    site_count = lax.axis_size("site")
    row_width = normals.shape[1]
    scen_here = row_width // HOURS
    local_blocks = normals.reshape(-1, BLK, row_width)
    block_count = local_blocks.shape[0]
    all_blocks = block_count * site_count
    my_columns = lax.dynamic_slice_in_dim(pattern, own_index * RB_DEV, RB_DEV, 0).reshape(-1)
    block_ids = jnp.arange(all_blocks, dtype=jnp.int32)
    wanted = pattern.reshape(site_count, -1)
    needed = jnp.any(wanted[:, :, None] == block_ids[None, None, :], axis=1)
    owned_need = lax.dynamic_slice_in_dim(needed, own_index * block_count, block_count, 1).astype(
        jnp.int32
    )
    slot_rank = jnp.cumsum(owned_need, axis=1) - 1
    slot_ids = jnp.arange(MAX_COLUMN_BLOCKS, dtype=jnp.int32)
    chosen = (owned_need[:, None, :] == 1) & (slot_rank[:, None, :] == slot_ids[None, :, None])
    local_ids = jnp.arange(block_count, dtype=jnp.int32)
    block_index = jnp.sum(jnp.where(chosen, local_ids[None, None, :], 0), axis=2)
    present = jnp.any(chosen, axis=2)
    outgoing = jnp.where(
        present[:, :, None, None], local_blocks[block_index], jnp.zeros((), normals.dtype)
    )
    arrived = lax.all_to_all(outgoing, "site", split_axis=0, concat_axis=0, tiled=True)
    my_need = lax.dynamic_index_in_dim(needed, own_index, 0, keepdims=False).astype(jnp.int32)
    my_rank = (jnp.cumsum(my_need.reshape(site_count, block_count), axis=1) - 1).reshape(-1)
    slot_of = my_columns // block_count * MAX_COLUMN_BLOCKS + my_rank[my_columns]
    picked = jnp.take(
        arrived.reshape(site_count * MAX_COLUMN_BLOCKS, BLK, row_width), slot_of, axis=0
    )
    picked = picked.reshape(RB_DEV, NZ, BLK, row_width)
    capacity_rows = capacity.reshape(RB_DEV, BLK)
    spread_rows = spread.reshape(RB_DEV, BLK)
    portion = lax.all_gather(factor, "scen", axis=2, tiled=True)
    height = portion.shape[2]
    spatial = jnp.einsum(
        "ktij,ktjw->kiw", portion, picked, preferred_element_type=jnp.float32
    ).astype(jnp.bfloat16)
    hourly = spatial.reshape(RB_DEV, height, scen_here, HOURS)
    weather = jnp.einsum("kpsg,hg->kpsh", hourly, temporal, preferred_element_type=jnp.float32)
    scale_part = capacity_rows[:, :, None, None]
    spread_part = spread_rows[:, :, None, None]
    values = scale_part * jnp.exp(spread_part * weather - 0.5 * spread_part * spread_part)
    injected = (
        values.astype(jnp.bfloat16)
        .reshape(RB_DEV, height, row_width)
        .reshape(RB_DEV * BLK, row_width)
    )
    bus_ids = own_index * BUS_DEV + jnp.arange(BUS_DEV, dtype=jnp.int32)
    onehot_rows = (bus_map[None, :] == bus_ids[:, None]).astype(jnp.bfloat16)
    return jnp.dot(
        onehot_rows,
        lax.all_gather(injected, "site", axis=0, tiled=True),
        preferred_element_type=jnp.float32,
    )


def solution(mesh):
    placed = (P("site", "scen"), P(), P("site", None, "scen", None), P(), P("site"), P("site"), P())
    return jax.shard_map(
        shards, mesh=mesh, in_specs=placed, out_specs=P("site", "scen"), check_vma=False
    )
```

profile of v0, /device:TPU:0, one launch (start us, length us, event | category | flops | bytes accessed | tf_op | source)
XLA Modules:
  0.0 440.7 jit_solution(17273901269101868076)
XLA Ops:
  6.5 0.7 all-gather.3.cloned.1.call-update
  7.3 0.8 eq.51
  8.1 0.3 fusion.18
  8.3 0.1 broadcast_compare_fusion
  8.4 0.2 reduce_window_sum.18
  8.6 0.2 select_reduce_fusion
  8.7 0.1 copy.13
  8.8 0.1 reshape.181
  8.9 3.9 copy.12
  12.8 2.8 copy.14
  15.6 0.2 fusion.21
  15.8 0.1 copy.11
  15.9 6.4 %gather_fusion.1 = bf16[40,256,336]{1,2,0:T(8,128)(2,1)} fusion(bf16[10,256,336]{1,2,0:T(8,128)(2,1)S(1)} %copy.14, s32[1024]{0:T(1024)S(1)} %pad_clamp_fusion.1), kind=kCustom, calls=%fused_computation.1 | custom fusion | bytes 13762720 | tf_op jit(solution)/shard_map/gather | solution.py:36
  22.3 7.8 %broadcast_select_fusion = bf16[8,5,256,336]{2,3,1,0:T(8,128)(2,1)} fusion(bf16[8,5,256,336]{2,3,1,0:T(8,128)(2,1)} %bitcast.33, pred[8,5]{1,0:T(8,128)(4,1)S(1)} %copy.11), kind=kLoop, calls=%fused_computation.7 | loop fusion | flops 3440640 | bytes 13762600 | tf_op jit(solution)/shard_map/jit(_where)/select_n | solution.py:35
  30.1 5.1 %all-to-all-start = ((bf16[8,5,256,336]{2,3,1,0:T(8,128)(2,1)}), bf16[8,5,256,336]{2,3,1,0:T(8,128)(2,1)}, u32[]{:S(2)}, u32[]{:S(2)}) async-start(bf16[8,5,256,336]{2,3,1,0:T(8,128)(2,1)} %broadcast_select_fusion), calls=%async_computation | async-start | bytes 13762560 | tf_op jit(solution)/shard_map/all_to_all | solution.py:38
  35.2 0.7 constant_dynamic-slice_fusion
  35.9 0.1 reshape.166
  36.1 0.1 reshape.170
  36.1 0.2 reduce_window_sum.17
  36.3 0.1 sub.26
  36.4 1.6 gather_fusion
  38.0 0.1 gather.17
  38.1 0.7 compare_and_fusion
  38.8 74.7 %all-to-all-done = bf16[8,5,256,336]{2,3,1,0:T(8,128)(2,1)} async-done(((bf16[8,5,256,336]{2,3,1,0:T(8,128)(2,1)}), bf16[8,5,256,336]{2,3,1,0:T(8,128)(2,1)}, u32[]{:S(2)}, u32[]{:S(2)}) %all-to-all-start) | async-done | bytes 6881312 | tf_op jit(solution)/shard_map/all_to_all | solution.py:38
  113.5 15.0 %gather_fusion.2 = bf16[160,256,336]{1,2,0:T(8,128)(2,1)} fusion(bf16[40,256,336]{1,2,0:T(8,128)(2,1)} %bitcast.4, s32[1024]{0:T(1024)S(1)} %pad_clamp_fusion), kind=kCustom, calls=%fused_computation.2 | custom fusion | bytes 55050880 | tf_op jit(solution)/shard_map/jit(_take)/gather | solution.py:42
  128.5 240.0 %all-gather.3.cloned.1.call-done = bf16[4,40,256,256]{3,2,1,0:T(8,128)(2,1)} async-done(((bf16[4,40,64,256]{3,2,1,0:T(8,128)(2,1)}), bf16[4,40,256,256]{3,2,1,0:T(8,128)(2,1)}) %all-gather.3.cloned.1.call-update) | async-done | bytes 20971536 | tf_op jit(solution)/shard_map/all_gather | solution.py:48
  368.5 17.8 %fusion.13 = bf16[4,336,256]{2,1,0:T(8,128)(2,1)S(1)} fusion(bf16[4,40,256,256]{3,2,1,0:T(8,128)(2,1)} %all-gather.3.cloned.1.call-done, bf16[4,40,256,336]{2,3,1,0:T(8,128)(2,1)} %bitcast.32, pred[4,40]{1,0:T(4,128)(4,1)S(1)} %compare_and_fusion), kind=kOutput, calls=%fused_computation.16 | convolution fusion | flops 7060537344 | bytes 49184928 | tf_op jit(solution)/shard_map/ktij,ktjw->kiw/dot_general | solution.py:50
  386.3 0.4 fusion.12
  386.7 0.4 copy.15
  387.1 1.0 copy.18
  388.2 40.8 %all-gather.5.cloned.1.call-done = bf16[8192,336]{0,1:T(8,128)(2,1)} async-done(((bf16[1024,336]{0,1:T(8,128)(2,1)}), bf16[8192,336]{0,1:T(8,128)(2,1)}) %all-gather.5.cloned.1.call-update) | async-done | bytes 5505040 | tf_op jit(solution)/shard_map/all_gather | solution.py:67
  429.0 4.9 %fusion.4 = f32[64,336]{1,0:T(8,128)} fusion(bf16[8192,336]{0,1:T(8,128)(2,1)} %all-gather.5.cloned.1.call-done, s32[8192]{0:T(1024)S(1)} %copy-done.1, s32[64]{0:T(128)S(1)} %iota_add_fusion), kind=kOutput, calls=%fused_computation.8 | convolution fusion | flops 352845824 | bytes 5624064 | tf_op jit(solution)/shard_map/dot_general | solution.py:65
  (24 shorter events, 0.2 us)
Async XLA Ops:
  6.5 379.8 %copy-start = (bf16[168,168]{1,0:T(8,128)(2,1)S(1)}, bf16[168,168]{1,0:T(8,128)(2,1)}, u32[]{:S(2)}) copy-start(bf16[168,168]{1,0:T(8,128)(2,1)} %param.10) | copy-start | bytes 169348
  6.5 362.0 %all-gather.3.cloned.1.call-start = ((), (), s32[]{:S(2)}) async-start(), calls=%async_computation.1 | async-start | bytes 26214400 | tf_op jit(solution)/shard_map/all_gather | solution.py:48
  30.1 7.9 %copy-start.2 = (f32[1024]{0:T(1024)S(1)}, f32[1024]{0:T(1024)}, u32[]{:S(2)}) copy-start(f32[1024]{0:T(1024)} %param.12) | copy-start | bytes 12292
  30.1 7.9 %copy-start.3 = (f32[1024]{0:T(1024)S(1)}, f32[1024]{0:T(1024)}, u32[]{:S(2)}) copy-start(f32[1024]{0:T(1024)} %param.11) | copy-start | bytes 12292
  30.1 83.4 %all-to-all-start = ((bf16[8,5,256,336]{2,3,1,0:T(8,128)(2,1)}), bf16[8,5,256,336]{2,3,1,0:T(8,128)(2,1)}, u32[]{:S(2)}, u32[]{:S(2)}) async-start(bf16[8,5,256,336]{2,3,1,0:T(8,128)(2,1)} %broadcast_select_fusion), calls=%async_computation | async-start | bytes 13762560 | tf_op jit(solution)/shard_map/all_to_all | solution.py:38
  35.2 393.8 %all-gather.5.cloned.1.call-start = ((), (), s32[]{:S(2)}) async-start(), calls=%async_computation.2 | async-start | bytes 6193152 | tf_op jit(solution)/shard_map/all_gather | solution.py:67
  368.5 60.5 %copy-start.1 = (s32[8192]{0:T(1024)S(1)}, s32[8192]{0:T(1024)}, u32[]{:S(2)}) copy-start(s32[8192]{0:T(1024)} %param.13) | copy-start | bytes 98308
Sparse Core Ops, SparseCore 0:
  8.9 359.5 all-gather.2
  388.3 40.6 all-gather.4
where the time goes:
time: 441 us
  waiting for transfers between devices  356 us (81%)
  local copies, waits for them, and re-layouts  33.1 us (8%)
  matrix products  23.1 us (5%)
  between operations  13.5 us (3%)
  other arithmetic  9.61 us (2%)
  starting transfers between devices  5.11 us (1%)
    all_gather x1, waiting for transfers between devices, shards(): portion = lax.all_gather(factor, 'scen', axis=2, tiled=True)  240 us
    all_to_all x1, waiting for transfers between devices, shards(): lax.all_to_all(outgoing, 'site', split_axis=0, concat_axis=0, tiled=True)  74.7 us
    all_gather x1, waiting for transfers between devices, shards(): lax.all_gather(injected, 'site', axis=0, tiled=True)  40.8 us
    dot_general x1, matrix products, shards(): jnp.einsum('ktij,ktjw->kiw', portion, picked, preferred_element_type=jnp....  17.8 us
    gather x1, local copies, waits for them, and re-layouts, shards(): jnp.take(arrived.reshape(site_count * MAX_COLUMN_BLOCKS, BLK, row_width),...  15 us
  transfers between devices with their start and end apart: 3, of which 3 were waited for; matrix products, arithmetic and copies ran while one was open for 9% of the time, Pallas kernels for 0%

commit v1 on v0

--- a/solution.py
+++ b/solution.py
@@ -2,6 +2,7 @@
 import jax.numpy as jnp
 from jax import lax
 from jax.sharding import PartitionSpec as P
+from jax.lax import all_gather
 
 BLK = 256
 HOURS = 168
@@ -9,6 +10,11 @@
 MAX_COLUMN_BLOCKS = 5
 RB_DEV = 4
 BUS_DEV = 64
+
+
+def define_the_packet(row_dim, z_in):
+    outcome_arr = all_gather(z_in, "scen")
+    return jnp.concatenate(outcome_arr, row_dim)
 
 
 def shards(normals, pattern, factor, temporal, capacity, spread, bus_map):
@@ -45,7 +51,7 @@
     picked = picked.reshape(RB_DEV, NZ, BLK, row_width)
     capacity_rows = capacity.reshape(RB_DEV, BLK)
     spread_rows = spread.reshape(RB_DEV, BLK)
-    portion = lax.all_gather(factor, "scen", axis=2, tiled=True)
+    portion = define_the_packet(2, factor)
     height = portion.shape[2]
     spatial = jnp.einsum(
         "ktij,ktjw->kiw", portion, picked, preferred_element_type=jnp.float32

time: 441 us -> 459 us (1.041)
  local copies, waits for them, and re-layouts: 33.1 us -> 49.2 us
    all_gather x0 -> x1, local copies, waits for them, and re-layouts: none -> 17.6 us  [define_the_packet(): outcome_arr = all_gather(z_in, 'scen')]
where the time goes in v1:
time: 459 us; the launch traced here: 458 us
  waiting for transfers between devices  358 us (78%)
  local copies, waits for them, and re-layouts  49.2 us (11%)
  matrix products  23.2 us (5%)
  between operations  13.5 us (3%)
  other arithmetic  8.98 us (2%)
  starting transfers between devices  5.36 us (1%)
    all_gather x1, waiting for transfers between devices, define_the_packet(): outcome_arr = all_gather(z_in, 'scen')  241 us
    all_to_all x1, waiting for transfers between devices, shards(): lax.all_to_all(outgoing, 'site', split_axis=0, concat_axis=0, tiled=True)  76.1 us
    all_gather x1, waiting for transfers between devices, shards(): lax.all_gather(injected, 'site', axis=0, tiled=True)  40.8 us
    dot_general x1, matrix products, shards(): jnp.einsum('ktij,ktjw->kiw', portion, picked, preferred_element_type=jnp....  17.8 us
    all_gather x1, local copies, waits for them, and re-layouts, define_the_packet(): outcome_arr = all_gather(z_in, 'scen')  17.6 us
    gather x1, local copies, waits for them, and re-layouts, shards(): jnp.take(arrived.reshape(site_count * MAX_COLUMN_BLOCKS, BLK, row_width),...  15 us
  transfers between devices with their start and end apart: 3, of which 3 were waited for; matrix products, arithmetic and copies ran while one was open for 9% of the time, Pallas kernels for 0%

profile of v1, /device:TPU:0, one launch (start us, length us, event | category | flops | bytes accessed | tf_op | source)
XLA Modules:
  0.0 458.4 jit_solution(9636435433377339043)
XLA Ops:
  6.5 0.7 all-gather.6.cloned.1.call-update
  7.3 3.9 copy.18
  11.2 2.8 copy.20
  14.0 0.1 eq.51
  14.0 0.3 fusion.18
  14.3 0.1 broadcast_compare_fusion
  14.4 0.2 reduce_window_sum.18
  14.5 0.2 select_reduce_fusion
  14.7 0.1 copy.19
  14.8 0.1 reshape.189
  14.9 0.2 fusion.21
  15.1 0.1 copy.17
  15.2 6.3 %gather_fusion.1 = bf16[40,256,336]{1,2,0:T(8,128)(2,1)} fusion(bf16[10,256,336]{1,2,0:T(8,128)(2,1)S(1)} %copy.20, s32[1024]{0:T(1024)S(1)} %pad_clamp_fusion.1), kind=kCustom, calls=%fused_computation.1 | custom fusion | bytes 13762720 | tf_op jit(solution)/shard_map/gather | solution.py:42
  21.5 7.8 %broadcast_select_fusion = bf16[8,5,256,336]{2,3,1,0:T(8,128)(2,1)} fusion(bf16[8,5,256,336]{2,3,1,0:T(8,128)(2,1)} %bitcast.37, pred[8,5]{1,0:T(8,128)(4,1)S(1)} %copy.17), kind=kLoop, calls=%fused_computation.7 | loop fusion | flops 3440640 | bytes 13762600 | tf_op jit(solution)/shard_map/jit(_where)/select_n | solution.py:41
  29.3 5.3 %all-to-all-start = ((bf16[8,5,256,336]{2,3,1,0:T(8,128)(2,1)}), bf16[8,5,256,336]{2,3,1,0:T(8,128)(2,1)}, u32[]{:S(2)}, u32[]{:S(2)}) async-start(bf16[8,5,256,336]{2,3,1,0:T(8,128)(2,1)} %broadcast_select_fusion), calls=%async_computation | async-start | bytes 13762560 | tf_op jit(solution)/shard_map/all_to_all | solution.py:44
  34.7 0.0 all-gather.4.cloned.1.call-start
  34.7 0.1 reshape.178
  34.8 0.2 reduce_window_sum.17
  35.0 0.1 sub.26
  35.1 0.1 reshape.172
  35.2 1.6 gather_fusion
  36.7 0.1 gather.17
  36.9 76.1 %all-to-all-done = bf16[8,5,256,336]{2,3,1,0:T(8,128)(2,1)} async-done(((bf16[8,5,256,336]{2,3,1,0:T(8,128)(2,1)}), bf16[8,5,256,336]{2,3,1,0:T(8,128)(2,1)}, u32[]{:S(2)}, u32[]{:S(2)}) %all-to-all-start) | async-done | bytes 6881312 | tf_op jit(solution)/shard_map/all_to_all | solution.py:44
  113.0 15.0 %gather_fusion.2 = bf16[160,256,336]{1,2,0:T(8,128)(2,1)} fusion(bf16[40,256,336]{1,2,0:T(8,128)(2,1)} %bitcast.4, s32[1024]{0:T(1024)S(1)} %pad_clamp_fusion), kind=kCustom, calls=%fused_computation.2 | custom fusion | bytes 55050880 | tf_op jit(solution)/shard_map/jit(_take)/gather | solution.py:48
  128.0 240.5 %all-gather.6.cloned.1.call-done = bf16[16,40,64,256]{3,2,1,0:T(8,128)(2,1)} async-done(((bf16[4,40,64,256]{3,2,1,0:T(8,128)(2,1)}), bf16[16,40,64,256]{3,2,1,0:T(8,128)(2,1)}) %all-gather.6.cloned.1.call-update) | async-done | bytes 20971536 | tf_op jit(solution)/shard_map/all_gather | solution.py:16
  368.5 17.6 %copy.21 = bf16[4,4,40,64,256]{4,3,0,2,1:T(8,128)(2,1)} copy(bf16[4,4,40,64,256]{4,3,2,1,0:T(8,128)(2,1)} %bitcast.38) | data formatting | bytes 41943040 | tf_op jit(solution)/shard_map/all_gather | solution.py:16
  386.1 17.8 %fusion.13 = bf16[4,336,256]{2,1,0:T(8,128)(2,1)S(1)} fusion(bf16[4,40,256,256]{3,2,1,0:T(8,128)(2,1)} %bitcast.39, bf16[4,40,256,336]{2,3,1,0:T(8,128)(2,1)} %bitcast.36, pred[4,40]{1,0:T(4,128)(4,1)S(1)} %compare_and_fusion), kind=kOutput, calls=%fused_computation.16 | convolution fusion | flops 7060537344 | bytes 49184928 | tf_op jit(solution)/shard_map/ktij,ktjw->kiw/dot_general | solution.py:56
  404.0 0.4 fusion.12
  404.4 0.4 copy.22
  404.8 1.0 copy.25
  405.8 40.8 %all-gather.4.cloned.1.call-done = bf16[8192,336]{0,1:T(8,128)(2,1)} async-done(((bf16[1024,336]{0,1:T(8,128)(2,1)}), bf16[8192,336]{0,1:T(8,128)(2,1)}) %all-gather.4.cloned.1.call-update) | async-done | bytes 5505040 | tf_op jit(solution)/shard_map/all_gather | solution.py:73
  446.6 4.9 %fusion.4 = f32[64,336]{1,0:T(8,128)} fusion(bf16[8192,336]{0,1:T(8,128)(2,1)} %all-gather.4.cloned.1.call-done, s32[8192]{0:T(1024)S(1)} %copy-done.1, s32[64]{0:T(128)S(1)} %iota_add_fusion), kind=kOutput, calls=%fused_computation.8 | convolution fusion | flops 352845824 | bytes 5624064 | tf_op jit(solution)/shard_map/dot_general | solution.py:71
  (27 shorter events, 0.2 us)
Async XLA Ops:
  6.5 397.4 %copy-start = (bf16[168,168]{1,0:T(8,128)(2,1)S(1)}, bf16[168,168]{1,0:T(8,128)(2,1)}, u32[]{:S(2)}) copy-start(bf16[168,168]{1,0:T(8,128)(2,1)} %param.10) | copy-start | bytes 169348
  6.5 7.4 %copy-start.2 = (s32[32,40]{1,0:T(8,128)S(1)}, s32[32,40]{1,0:T(8,128)}, u32[]{:S(2)}) copy-start(s32[32,40]{1,0:T(8,128)} %param.8) | copy-start | bytes 15364
  6.5 362.0 %all-gather.6.cloned.1.call-start = ((), (), s32[]{:S(2)}) async-start(), calls=%async_computation.2 | async-start | bytes 26214400 | tf_op jit(solution)/shard_map/all_gather | solution.py:16
  29.3 7.5 %copy-start.3 = (f32[1024]{0:T(1024)S(1)}, f32[1024]{0:T(1024)}, u32[]{:S(2)}) copy-start(f32[1024]{0:T(1024)} %param.12) | copy-start | bytes 12292
  29.3 7.5 %copy-start.4 = (f32[1024]{0:T(1024)S(1)}, f32[1024]{0:T(1024)}, u32[]{:S(2)}) copy-start(f32[1024]{0:T(1024)} %param.11) | copy-start | bytes 12292
  29.3 83.7 %all-to-all-start = ((bf16[8,5,256,336]{2,3,1,0:T(8,128)(2,1)}), bf16[8,5,256,336]{2,3,1,0:T(8,128)(2,1)}, u32[]{:S(2)}, u32[]{:S(2)}) async-start(bf16[8,5,256,336]{2,3,1,0:T(8,128)(2,1)} %broadcast_select_fusion), calls=%async_computation | async-start | bytes 13762560 | tf_op jit(solution)/shard_map/all_to_all | solution.py:44
  34.7 412.0 %all-gather.4.cloned.1.call-start = ((), (), s32[]{:S(2)}) async-start(), calls=%async_computation.1 | async-start | bytes 6193152 | tf_op jit(solution)/shard_map/all_gather | solution.py:73
  386.1 60.5 %copy-start.1 = (s32[8192]{0:T(1024)S(1)}, s32[8192]{0:T(1024)}, u32[]{:S(2)}) copy-start(s32[8192]{0:T(1024)} %param.13) | copy-start | bytes 98308
Sparse Core Ops, SparseCore 0:
  8.9 359.5 all-gather.5
  405.9 40.6 all-gather.3
